TPU v7x, 256 devices: a whole 4x4x8 slice. The times are simulated.
256 devices in a mesh: dp: 64 (over z, x, core), rep: 4 (over y).
Axes of the slice: x: 4, y: 4, z: 8, core: 2. Of those that a mesh axis runs over, the one named last changes fastest.
Arguments:
- ecg: bfloat16 [4, 327680], P('rep', 'dp'), may hold values from -6 to 6
- conv_first: bfloat16 [5, 256], replicated, may hold values from -2.5 to 2.5
- conv_second: bfloat16 [512, 256], replicated, may hold values from -0.25 to 0.25
- conv_third: bfloat16 [512, 256], replicated, may hold values from -0.25 to 0.25
- enc_gain: float32 [256], replicated, may hold values from 0.1 to 1.9
- ctx_weight: bfloat16 [2, 512, 256], replicated, may hold values from -0.25 to 0.25
- head_weight: bfloat16 [256, 12, 256], replicated, may hold values from -0.375 to 0.375
- sources: int32 [4, 512, 4, 2], P('rep', 'dp'), may hold values from 0 to 63, as said below
Outputs:
- target_grad: float32 [4, 16384, 256], P('rep', 'dp')
- head_grad: float32 [4, 256, 12, 256], P('rep')
Inputs may be any that keep to these rules, and one draw needn't show every extreme that they name: sources[r, i, s] = (o, b): o is the piece index along the recording, b a block of 128 rows of that piece's 256 positions. Among the 32 entries of one piece at most 2 name the same piece o, and in every draw one piece o is named exactly 2 times by every piece of its recording.
All inputs are finite; a program needn't handle non-finite values.
Results may differ from a plain program's by a relative error of at most 0.0085.
Values may be sent and summed in bfloat16 or wider, within the bound.
No kernel may reach another device: no remote copies, remote signals or barrier semaphores. Data moves between devices by JAX's collectives and lax.ppermute only.
A program may use at most 128 MiB of HBM per device.

v0:
```python
import math
import jax
import jax.numpy as jnp
from jax import lax
from jax.sharding import PartitionSpec as P


def gelu_exact(values):
    return jax.nn.gelu(values, approximate=False)


def encode(piece, conv_first, conv_second, conv_third, enc_gain, ctx_weight):
    channels = conv_first.shape[1]
    positions = piece.shape[0] // 20
    frames = piece.reshape(4 * positions, 5)
    hidden_one = gelu_exact(jnp.dot(frames, conv_first, preferred_element_type=jnp.float32)).astype(
        jnp.bfloat16
    )
    hidden_two = gelu_exact(
        jnp.dot(
            hidden_one.reshape(2 * positions, 2 * channels),
            conv_second,
            preferred_element_type=jnp.float32,
        )
    ).astype(jnp.bfloat16)
    mixed = jnp.dot(
        hidden_two.reshape(positions, 2 * channels), conv_third, preferred_element_type=jnp.float32
    )
    average = jnp.mean(mixed, -1, keepdims=True)
    centred = mixed - average
    variance = jnp.mean(centred * centred, -1, keepdims=True)
    latent = (centred / jnp.sqrt(variance + 1e-05) * enc_gain).astype(jnp.bfloat16)
    latent_wide = latent.astype(jnp.float32)
    target = (
        latent_wide / jnp.sqrt(jnp.sum(latent_wide * latent_wide, -1, keepdims=True) + 1e-06)
    ).astype(jnp.bfloat16)
    context = latent
    for layer_index in range(ctx_weight.shape[0]):
        dilation = 2**layer_index
        before = jnp.concatenate(
            [jnp.zeros((dilation, channels), jnp.bfloat16), context[: positions - dilation]], 0
        )
        joined = jnp.concatenate([context, before], 1)
        update = gelu_exact(
            jnp.dot(joined, ctx_weight[layer_index], preferred_element_type=jnp.float32)
        )
        context = (context.astype(jnp.float32) + update).astype(jnp.bfloat16)
    return (target, context)


def score_piece(target, context, head_weight, negatives):
    positions, channels = target.shape
    horizon = head_weight.shape[1]
    groups = negatives.shape[0]
    pred = jnp.dot(
        context,
        head_weight.reshape(channels, horizon * channels),
        preferred_element_type=jnp.float32,
    ).reshape(positions, horizon, channels)
    pred_norm = jnp.sqrt(jnp.sum(pred * pred, -1, keepdims=True) + 1e-06)
    unit_pred = pred / pred_norm
    queries = unit_pred.astype(jnp.bfloat16)
    shifted = jnp.stack(
        [
            jnp.concatenate(
                [target[step_index + 1 :], jnp.zeros((step_index + 1, channels), jnp.bfloat16)], 0
            )
            for step_index in range(horizon)
        ],
        1,
    )
    usable = (
        lax.broadcasted_iota(jnp.int32, (positions, horizon), 0)
        + lax.broadcasted_iota(jnp.int32, (positions, horizon), 1)
        + 1
        < positions
    ).astype(jnp.float32)
    positive = 10.0 * jnp.sum(queries.astype(jnp.float32) * shifted.astype(jnp.float32), -1)
    grouped = queries.reshape(groups, -1, channels)
    negative = 10.0 * jnp.einsum(
        "gqc,gnc->gqn", grouped, negatives, preferred_element_type=jnp.float32
    )
    pos_exp = jnp.exp(positive)
    neg_exp = jnp.exp(negative)
    partition = pos_exp.reshape(groups, -1) + jnp.sum(neg_exp, -1)
    usable_grouped = usable.reshape(groups, -1)
    pos_weight = 10.0 * usable * (pos_exp / partition.reshape(positions, horizon) - 1.0)
    neg_weight = (10.0 * usable_grouped[:, :, None] * neg_exp / partition[:, :, None]).astype(
        jnp.bfloat16
    )
    neg_part = jnp.einsum("gqn,gnc->gqc", neg_weight, negatives, preferred_element_type=jnp.float32)
    query_grad = pos_weight[:, :, None] * shifted.astype(jnp.float32) + neg_part.reshape(
        positions, horizon, channels
    )
    neg_grad = jnp.einsum(
        "gqn,gqc->gnc", neg_weight, grouped, preferred_element_type=jnp.float32
    ).astype(jnp.bfloat16)
    pos_terms = pos_weight[:, :, None] * queries.astype(jnp.float32)
    pos_grad = jnp.zeros((positions, channels), jnp.float32)
    for step_index in range(horizon):
        moved = jnp.concatenate(
            [
                jnp.zeros((step_index + 1, channels), jnp.float32),
                pos_terms[: positions - step_index - 1, step_index],
            ],
            0,
        )
        pos_grad = pos_grad + moved
    radial = jnp.sum(unit_pred * query_grad, -1, keepdims=True)
    pred_grad = (
        ((query_grad - unit_pred * radial) / pred_norm)
        .astype(jnp.bfloat16)
        .reshape(positions, horizon * channels)
    )
    head_part = lax.dot_general(
        context, pred_grad, (((0,), (0,)), ((), ())), preferred_element_type=jnp.float32
    )
    return (pos_grad, neg_grad, head_part)


def local(ecg, conv_first, conv_second, conv_third, enc_gain, ctx_weight, head_weight, sources):
    owner_total = lax.axis_size("dp")
    groups = sources.shape[1]
    entries = sources.reshape(-1, 2)
    owner_id = entries[:, 0]
    block_id = entries[:, 1]
    entry_count = entries.shape[0]
    capacity = max(2, 2 * entry_count // owner_total)
    slot_total = owner_total * capacity
    earlier = lax.broadcasted_iota(jnp.int32, (entry_count, entry_count), 1) < lax.broadcasted_iota(
        jnp.int32, (entry_count, entry_count), 0
    )
    same_owner = owner_id[:, None] == owner_id[None, :]
    rank_of = jnp.sum((earlier & same_owner).astype(jnp.int32), 1)
    slot_of = owner_id * capacity + rank_of
    matches = slot_of[:, None] == jnp.arange(slot_total, dtype=jnp.int32)[None, :]
    wanted = jnp.sum(jnp.where(matches, block_id[:, None], 0), 0).reshape(owner_total, capacity)
    occupied = jnp.any(matches, 0)
    entry_of = jnp.sum(jnp.where(matches, jnp.arange(entry_count, dtype=jnp.int32)[:, None], 0), 0)
    requested = lax.all_to_all(wanted, "dp", split_axis=0, concat_axis=0, tiled=True)
    target, context = encode(
        ecg.reshape(-1), conv_first, conv_second, conv_third, enc_gain, ctx_weight
    )
    positions, channels = target.shape
    segment = lax.all_gather(target, "dp", axis=0, tiled=True)
    piece_count = segment.shape[0] // positions
    segment_blocks = segment.reshape(piece_count, positions // 128, 128, channels)
    chosen = jnp.take_along_axis(segment_blocks, wanted[:, :, None, None], axis=1)
    chosen = chosen.reshape(piece_count * capacity, 128, channels)
    fetched = jnp.take(chosen, slot_of, axis=0)
    negatives = fetched.reshape(groups, -1, channels)
    pos_grad, neg_grad, head_part = score_piece(target, context, head_weight, negatives)
    horizon = head_weight.shape[1]
    neg_blocks = neg_grad.reshape(entry_count, 128, channels)
    picked = jnp.take(neg_blocks, entry_of, axis=0)
    outgoing = jnp.where(occupied[:, None, None], picked, jnp.zeros_like(picked)).reshape(
        owner_total, capacity, 128, channels
    )
    returned = lax.all_to_all(outgoing, "dp", split_axis=0, concat_axis=0, tiled=True).reshape(
        slot_total, 128 * channels
    )
    placed = (
        requested.reshape(-1)[None, :] == jnp.arange(positions // 128, dtype=jnp.int32)[:, None]
    ).astype(jnp.bfloat16)
    summed = jnp.dot(placed, returned, preferred_element_type=jnp.float32).reshape(
        positions, channels
    )
    target_grad = ((pos_grad + summed) / horizon)[None]
    head_total = lax.psum(head_part, "dp")
    factor = math.sqrt(channels / (lax.axis_size("dp") * positions))
    head_grad = (head_total * factor).reshape(1, channels, horizon, channels)
    return (target_grad, head_grad)


def solution(mesh):
    in_specs = (P("rep", "dp"), P(), P(), P(), P(), P(), P(), P("rep", "dp", None, None))
    out_specs = (P("rep", "dp", None), P("rep", None, None, None))
    return jax.shard_map(local, mesh=mesh, in_specs=in_specs, out_specs=out_specs, check_vma=False)
```

profile of v0, /device:TPU:8, one launch (start us, length us, event | category | flops | bytes accessed | tf_op | source)
XLA Modules:
  0.0 485.1 jit_solution(15221614664519750533)
XLA Ops:
  7.2 0.8 reduce
  8.5 3.1 fusion.12
  11.8 1.3 fusion.22
  13.9 0.8 fusion.34
  15.3 0.7 all_to_all.9
  16.0 12.7 %all-to-all-start = ((s32[64,1,2]{2,1,0:T(1,128)}), s32[64,1,2]{2,1,0:T(1,128)}, u32[]{:S(2)}, u32[]{:S(2)}) async-start(s32[64,1,2]{2,1,0:T(1,128)} %bitcast.38), calls=%async_computation | async-start | bytes 65536 | tf_op jit(solution)/shard_map/all_to_all | solution.py:140
  28.8 1.6 slice.139
  30.4 1.6 slice.138
  32.0 1.6 slice.137
  33.6 1.6 slice.136
  35.2 1.6 slice.135
  36.7 0.9 slice.134
  37.7 1.6 slice.133
  39.3 1.6 slice.132
  40.8 1.6 slice.131
  42.4 1.6 slice.130
  44.0 1.6 slice.129
  47.1 0.8 broadcast_in_dim.116
  48.0 0.7 reduce_sum.109
  49.8 0.9 bitcast_dynamic-update-slice_fusion.11
  50.7 0.9 bitcast_dynamic-update-slice_fusion.10
  51.7 0.9 bitcast_dynamic-update-slice_fusion.9
  52.6 0.9 bitcast_dynamic-update-slice_fusion.8
  53.5 0.9 bitcast_dynamic-update-slice_fusion.7
  54.4 0.9 bitcast_dynamic-update-slice_fusion.6
  55.4 0.9 bitcast_dynamic-update-slice_fusion.4
  56.3 0.9 bitcast_dynamic-update-slice_fusion.3
  57.2 0.9 bitcast_dynamic-update-slice_fusion.2
  58.1 0.9 bitcast_dynamic-update-slice_fusion.1
  59.1 1.9 fusion.32
  61.0 0.7 fusion.40
  62.5 1.2 fusion.2
  64.2 1.2 copy-done.6
  65.4 2.3 copy.45
  67.7 2.5 reshape.248
  70.4 30.4 %all-gather.2.cloned.1.call-done = bf16[16384,256]{1,0:T(8,128)(2,1)} async-done(((bf16[256,256]{1,0:T(8,128)(2,1)}), bf16[16384,256]{1,0:T(8,128)(2,1)}) %all-gather.2.cloned.1.call-update) | async-done | bytes 8388624 | tf_op jit(solution)/shard_map/all_gather | solution.py:145
  100.8 10.6 %gather_fusion.2 = bf16[128,128,256]{2,1,0:T(8,128)(2,1)} fusion(bf16[64,2,128,256]{3,2,1,0:T(8,128)(2,1)} %bitcast.130, s32[128]{0:T(128)S(1)} %reshape.273), kind=kCustom, calls=%fused_computation.2 | custom fusion | bytes 16778240 | tf_op jit(solution)/shard_map/jit(take_along_axis)/gather | solution.py:148
  111.3 7.4 %broadcast_select_fusion = bf16[128,128,256]{2,1,0:T(8,128)(2,1)} fusion(bf16[128,128,256]{2,1,0:T(8,128)(2,1)} %gather_fusion.2, pred[128]{0:T(512)(128)(4,1)S(1)} %compare_and_fusion.1), kind=kLoop, calls=%fused_computation.5 | loop fusion | flops 4194304 | bytes 16777344 | tf_op jit(solution)/shard_map/jit(take_along_axis)/select_n | solution.py:148
  118.8 5.4 %gather_fusion = bf16[32,128,256]{2,1,0:T(8,128)(2,1)} fusion(bf16[128,128,256]{2,1,0:T(8,128)(2,1)} %broadcast_select_fusion, s32[1024]{0:T(1024)S(1)} %get-tuple-element.29), kind=kCustom, calls=%fused_computation | custom fusion | bytes 4194432 | tf_op jit(solution)/shard_map/jit(_take)/gather | solution.py:150
  124.1 1.9 bitcast_select_fusion
  126.1 3.8 fusion.1
  130.4 3.8 divide_convert_fusion
  134.3 1.4 convolution_convert_fusion
  135.9 6.4 %gather_fusion.1 = bf16[128,128,256]{2,1,0:T(8,128)(2,1)} fusion(bf16[32,128,256]{2,1,0:T(8,128)(2,1)S(1)} %bitcast.125, s32[1024]{0:T(1024)S(1)} %get-tuple-element.28), kind=kCustom, calls=%fused_computation.1 | custom fusion | bytes 16777728 | tf_op jit(solution)/shard_map/jit(_take)/gather | solution.py:155
  142.3 7.4 %select_select_fusion = bf16[64,2,128,256]{3,2,1,0:T(8,128)(2,1)} fusion(bf16[64,2,128,256]{3,2,1,0:T(8,128)(2,1)} %bitcast.126, pred[64,2]{1,0:T(8,128)(4,1)S(1)} %compare_and_fusion, pred[64,2]{1,0:T(8,128)(4,1)S(1)} %copy-done.27), kind=kLoop, calls=%fused_computation.4 | loop fusion | flops 8388608 | bytes 16777472 | tf_op jit(solution)/shard_map/jit(_where)/select_n | solution.py:156
  149.7 6.9 %all-to-all-start.1 = ((bf16[64,2,128,256]{3,2,1,0:T(8,128)(2,1)}), bf16[64,2,128,256]{3,2,1,0:T(8,128)(2,1)}, u32[]{:S(2)}, u32[]{:S(2)}) async-start(bf16[64,2,128,256]{3,2,1,0:T(8,128)(2,1)} %select_select_fusion), calls=%async_computation.1 | async-start | bytes 16777216 | tf_op jit(solution)/shard_map/all_to_all | solution.py:159
  157.2 1.5 reduce.8
  158.8 4.2 fusion.105
  163.0 4.8 reshape.254
  167.8 21.8 %divide_convert_fusion.1 = bf16[256,12,256]{2,0,1:T(8,128)(2,1)} fusion(f32[256,12]{0,1:T(8,128)S(1)} %add_sqrt_fusion, f32[256,12,256]{2,1,0:T(8,128)} %reshape.254, bf16[256,12,256]{2,0,1:T(8,128)(2,1)} %copy-done.12, f32[256,12]{0,1:T(8,128)S(1)} %get-tuple-element.18, f32[256,12,256]{2,0,1:T(8,128)S(1)} %copy-done.11), kind=kOutput, calls=%fused_computation.14 | output fusion | flops 10226943 | bytes 9461760 | tf_op jit(solution)/shard_map/mul | solution.py:111
  189.7 1.7 copy.53
  191.4 2.3 fusion.106
  194.2 0.7 slice_bitcast_fusion.7
  195.6 0.7 slice_bitcast_fusion.9
  196.4 0.7 slice_bitcast_fusion.10
  199.3 0.7 slice_bitcast_fusion.2
  200.0 0.7 slice_bitcast_fusion.3
  202.8 247.4 %all-reduce.28.cloned.1.call-done = f32[256,3072]{1,0:T(8,128)} async-done(((f32[256,3072]{1,0:T(8,128)}), f32[256,3072]{1,0:T(8,128)}) %all-reduce.28.cloned.1.call-update) | async-done | bytes 3145744 | tf_op jit(solution)/shard_map/psum | solution.py:169
  450.3 2.1 broadcast_multiply_fusion
  452.4 2.3 copy.54
  454.7 3.7 copy.55
  458.5 12.3 %copy.58 = bf16[16,8,128,256]{3,1,2,0:T(8,128)(2,1)} copy(bf16[16,8,128,256]{3,2,1,0:T(8,128)(2,1)} %bitcast.52) | data formatting | bytes 16777216
  470.9 4.7 fusion.90
  476.0 2.1 multiply_bitcast_fusion
  (137 shorter events, 13.3 us)
Async XLA Ops:
  7.2 4.5 copy-start
  7.2 93.6 %all-gather.2.cloned.1.call-start = ((), (), s32[]{:S(2)}) async-start(), calls=%async_computation.2 | async-start | bytes 8519680 | tf_op jit(solution)/shard_map/all_gather | solution.py:145
  11.7 1.4 copy-start.25
  11.7 2.0 copy-start.35
  11.7 3.0 copy-start.30
  13.1 36.1 %copy-start.13 = (bf16[256,12,256]{2,0,1:T(8,128)(2,1)S(1)}, bf16[256,12,256]{2,0,1:T(8,128)(2,1)}, u32[]{:S(2)}) copy-start(bf16[256,12,256]{2,0,1:T(8,128)(2,1)} %param.14) | copy-start | bytes 4718596
  14.7 30.9 %copy-start.4 = (bf16[256,256]{1,0:T(8,128)(2,1)S(1)}, bf16[256,256]{1,0:T(8,128)(2,1)}, u32[]{:S(2)}) copy-start(bf16[256,256]{1,0:T(8,128)(2,1)} %fusion.34) | copy-start | bytes 393220
  15.1 33.7 %copy-start.33 = (s32[32,1]{0,1:T(1,128)}, s32[32,1]{0,1:T(1,128)S(1)}, u32[]{:S(2)}) copy-start(s32[32,1]{0,1:T(1,128)S(1)} %get-tuple-element.15) | copy-start | bytes 388
  15.2 19.9 %copy-start.28 = (s32[128]{0:T(128)}, s32[128]{0:T(128)S(1)}, u32[]{:S(2)}) copy-start(s32[128]{0:T(128)S(1)} %get-tuple-element.11) | copy-start | bytes 1540
  15.2 33.6 %copy-start.31 = (s32[128]{0:T(128)}, s32[128]{0:T(128)S(1)}, u32[]{:S(2)}) copy-start(s32[128]{0:T(128)S(1)} %get-tuple-element.10) | copy-start | bytes 1540
  16.0 133.7 %all-to-all-start = ((s32[64,1,2]{2,1,0:T(1,128)}), s32[64,1,2]{2,1,0:T(1,128)}, u32[]{:S(2)}, u32[]{:S(2)}) async-start(s32[64,1,2]{2,1,0:T(1,128)} %bitcast.38), calls=%async_computation | async-start | bytes 65536 | tf_op jit(solution)/shard_map/all_to_all | solution.py:140
  48.9 10.1 %copy-start.24 = (bf16[244,256]{1,0:T(8,128)(2,1)S(1)}, bf16[244,256]{1,0:T(8,128)(2,1)}, u32[]{:S(2)}) copy-start(bf16[244,256]{1,0:T(8,128)(2,1)} %slice.139) | copy-start | bytes 374788
  59.1 3.5 copy-start.12
  59.1 2.0 copy-start.37
  62.5 1.7 copy-start.10
  64.2 1.2 copy-start.6
  65.4 4.8 copy-start.34
  65.4 4.8 copy-start.32
  65.4 4.8 copy-start.29
  65.4 4.9 %copy-start.36 = (pred[8,4]{0,1:T(4,128)(4,1)S(1)}, pred[8,4]{0,1:T(4,128)(4,1)}, u32[]{:S(2)}) copy-start(pred[8,4]{0,1:T(4,128)(4,1)} %copy.47) | copy-start | bytes 100
  65.4 4.9 %copy-start.26 = (s32[64,2]{1,0:T(8,128)S(1)}, s32[64,2]{1,0:T(8,128)}, u32[]{:S(2)}) copy-start(s32[64,2]{1,0:T(8,128)} %reduce_sum.109) | copy-start | bytes 1540
  70.2 55.9 %copy-start.8 = (bf16[8,384,256]{2,1,0:T(8,128)(2,1)}, bf16[8,384,256]{2,1,0:T(8,128)(2,1)S(1)}, u32[]{:S(2)}) copy-start(bf16[8,384,256]{2,1,0:T(8,128)(2,1)S(1)} %reshape.248) | copy-start | bytes 4718596
  126.1 3.8 copy-start.5
  130.4 3.8 copy-start.9
  134.2 1.7 copy-start.2
  135.9 6.4 %copy-start.27 = (pred[64,2]{1,0:T(8,128)(4,1)S(1)}, pred[64,2]{1,0:T(8,128)(4,1)}, u32[]{:S(2)}) copy-start(pred[64,2]{1,0:T(8,128)(4,1)} %broadcast_in_dim.116) | copy-start | bytes 388
  149.7 9.1 %copy-start.3 = (bf16[8,384,512]{2,1,0:T(8,128)(2,1)S(1)}, bf16[8,384,512]{2,1,0:T(8,128)(2,1)}, u32[]{:S(2)}) copy-start(bf16[8,384,512]{2,1,0:T(8,128)(2,1)} %copy-done.2) | copy-start | bytes 9437188
  149.7 308.8 %all-to-all-start.1 = ((bf16[64,2,128,256]{3,2,1,0:T(8,128)(2,1)}), bf16[64,2,128,256]{3,2,1,0:T(8,128)(2,1)}, u32[]{:S(2)}, u32[]{:S(2)}) async-start(bf16[64,2,128,256]{3,2,1,0:T(8,128)(2,1)} %select_select_fusion), calls=%async_computation.1 | async-start | bytes 16777216 | tf_op jit(solution)/shard_map/all_to_all | solution.py:159
  156.6 293.7 %all-reduce.28.cloned.1.call-start = ((), (), s32[]{:S(2)}) async-start(), calls=%async_computation.3 | async-start | bytes 6291456 | tf_op jit(solution)/shard_map/psum | solution.py:169
  163.0 4.8 copy-start.11
  191.4 2.3 copy-start.7
  470.8 5.0 %copy-start.14 = (f32[249,256]{1,0:T(8,128)S(1)}, f32[249,256]{1,0:T(8,128)}, u32[]{:S(2)}) copy-start(f32[249,256]{1,0:T(8,128)} %slice_bitcast_fusion) | copy-start | bytes 764932
  470.8 5.1 %copy-start.15 = (f32[250,256]{1,0:T(8,128)S(1)}, f32[250,256]{1,0:T(8,128)}, u32[]{:S(2)}) copy-start(f32[250,256]{1,0:T(8,128)} %slice_bitcast_fusion.1) | copy-start | bytes 768004
  470.8 5.1 %copy-start.16 = (f32[251,256]{1,0:T(8,128)S(1)}, f32[251,256]{1,0:T(8,128)}, u32[]{:S(2)}) copy-start(f32[251,256]{1,0:T(8,128)} %slice_bitcast_fusion.2) | copy-start | bytes 771076
  470.8 5.1 %copy-start.17 = (f32[252,256]{1,0:T(8,128)S(1)}, f32[252,256]{1,0:T(8,128)}, u32[]{:S(2)}) copy-start(f32[252,256]{1,0:T(8,128)} %slice_bitcast_fusion.3) | copy-start | bytes 774148
  470.8 5.1 %copy-start.18 = (f32[253,256]{1,0:T(8,128)S(1)}, f32[253,256]{1,0:T(8,128)}, u32[]{:S(2)}) copy-start(f32[253,256]{1,0:T(8,128)} %slice_bitcast_fusion.4) | copy-start | bytes 777220
  470.8 5.1 %copy-start.19 = (f32[254,256]{1,0:T(8,128)S(1)}, f32[254,256]{1,0:T(8,128)}, u32[]{:S(2)}) copy-start(f32[254,256]{1,0:T(8,128)} %slice_bitcast_fusion.5) | copy-start | bytes 780292
  470.9 5.1 %copy-start.20 = (f32[255,256]{1,0:T(8,128)S(1)}, f32[255,256]{1,0:T(8,128)}, u32[]{:S(2)}) copy-start(f32[255,256]{1,0:T(8,128)} %slice_bitcast_fusion.6) | copy-start | bytes 783364
  470.9 5.1 %copy-start.21 = (f32[244,256]{1,0:T(8,128)S(1)}, f32[244,256]{1,0:T(8,128)}, u32[]{:S(2)}) copy-start(f32[244,256]{1,0:T(8,128)} %slice_bitcast_fusion.7) | copy-start | bytes 749572
  470.9 5.1 %copy-start.22 = (f32[245,256]{1,0:T(8,128)S(1)}, f32[245,256]{1,0:T(8,128)}, u32[]{:S(2)}) copy-start(f32[245,256]{1,0:T(8,128)} %slice_bitcast_fusion.8) | copy-start | bytes 752644
  470.9 5.1 %copy-start.23 = (f32[246,256]{1,0:T(8,128)S(1)}, f32[246,256]{1,0:T(8,128)}, u32[]{:S(2)}) copy-start(f32[246,256]{1,0:T(8,128)} %slice_bitcast_fusion.9) | copy-start | bytes 755716
  470.9 7.2 %copy-start.1 = (bf16[512,256]{1,0:T(8,128)(2,1)S(1)}, bf16[512,256]{1,0:T(8,128)(2,1)}, u32[]{:S(2)}) copy-start(bf16[512,256]{1,0:T(8,128)(2,1)} %param.10) | copy-start | bytes 786436
Sparse Core Ops, SparseCore 0:
  14.9 85.8 all-gather.1
  193.8 256.3 all-reduce.27
where the time goes:
time: 491 us; the launch traced here: 485 us
  waiting for transfers between devices  278 us (57%)
  local copies, waits for them, and re-layouts  95.8 us (20%)
  other arithmetic  52.4 us (11%)
  matrix products  24.5 us (5%)
  starting transfers between devices  19.6 us (4%)
  between operations  15.1 us (3%)
    psum x1, waiting for transfers between devices, local(): head_total = lax.psum(head_part, 'dp')  247 us
    all_gather x1, waiting for transfers between devices, local(): segment = lax.all_gather(target, 'dp', axis=0, tiled=True)  30.4 us
    unnamed x91, local copies, waits for them, and re-layouts  28.1 us
    mul x1, other arithmetic, score_piece(): unit_pred * radial  21.8 us
    slice x12, local copies, waits for them, and re-layouts, score_piece(): target[step_index + 1:]  17.5 us
    all_to_all x1, starting transfers between devices, local(): lax.all_to_all(wanted, 'dp', split_axis=0, concat_axis=0, tiled=True)  12.7 us
    gather x2, local copies, waits for them, and re-layouts, local(): jnp.take_along_axis(segment_blocks, wanted[:, :, None, None], axis=1)  10.7 us
  transfers between devices with their start and end apart: 4, of which 2 were waited for; matrix products, arithmetic and copies ran while one was open for 29% of the time, Pallas kernels for 0%

commit v1 on v0

--- a/solution.py
+++ b/solution.py
@@ -142,7 +142,10 @@
         ecg.reshape(-1), conv_first, conv_second, conv_third, enc_gain, ctx_weight
     )
     positions, channels = target.shape
-    segment = lax.all_gather(target, "dp", axis=0, tiled=True)
+    prepare_the_rings = lambda frame: jnp.concatenate(
+        lax.all_to_all(jnp.stack([frame] * lax.axis_size("dp")), "dp", 0, 0), axis=0
+    )
+    segment = prepare_the_rings(target)
     piece_count = segment.shape[0] // positions
     segment_blocks = segment.reshape(piece_count, positions // 128, 128, channels)
     chosen = jnp.take_along_axis(segment_blocks, wanted[:, :, None, None], axis=1)

time: 491 us -> 619 us (1.26)
  waiting for transfers between devices: 278 us -> 404 us
  starting transfers between devices: 19.6 us -> 30.6 us
  local copies, waits for them, and re-layouts: 95.8 us -> 88.2 us
    all_to_all x0 -> x1, waiting for transfers between devices: none -> 155 us  [local(): lax.all_to_all(jnp.stack([frame] * lax.axis_size('dp')), 'dp', 0, 0)]
    all_gather x1 -> x0, waiting for transfers between devices: 30.4 us -> none  [local(): segment = lax.all_gather(target, 'dp', axis=0, tiled=True)]
    all_to_all x0 -> x1, starting transfers between devices: none -> 12.6 us  [local(): lax.all_to_all(jnp.stack([frame] * lax.axis_size('dp')), 'dp', 0, 0)]
    slice x12 -> x13, local copies, waits for them, and re-layouts: 17.5 us -> 6.85 us  [score_piece(): target[step_index + 1:]]
    unnamed x91 -> x73, local copies, waits for them, and re-layouts: 28.1 us -> 27.1 us
  transfers between devices with their start and end apart: 4 -> 4, of which waited for: 2 -> 2; matrix products, arithmetic and copies ran while one was open for 29% -> 21% of each run, Pallas kernels for 0% -> 0%
where the time goes in v1:
time: 619 us; the launch traced here: 613 us
  waiting for transfers between devices  404 us (65%)
  local copies, waits for them, and re-layouts  88.2 us (14%)
  other arithmetic  50.8 us (8%)
  starting transfers between devices  30.6 us (5%)
  matrix products  24.5 us (4%)
  between operations  15 us (2%)
    psum x1, waiting for transfers between devices, local(): head_total = lax.psum(head_part, 'dp')  249 us
    all_to_all x1, waiting for transfers between devices, local(): lax.all_to_all(jnp.stack([frame] * lax.axis_size('dp')), 'dp', 0, 0)  155 us
    unnamed x73, local copies, waits for them, and re-layouts  27.1 us
    mul x1, other arithmetic, score_piece(): unit_pred * radial  21.9 us
    all_to_all x1, starting transfers between devices, local(): lax.all_to_all(jnp.stack([frame] * lax.axis_size('dp')), 'dp', 0, 0)  12.6 us
  transfers between devices with their start and end apart: 4, of which 2 were waited for; matrix products, arithmetic and copies ran while one was open for 21% of the time, Pallas kernels for 0%

profile of v1, /device:TPU:8, one launch (start us, length us, event | category | flops | bytes accessed | tf_op | source)
XLA Modules:
  0.0 612.6 jit_solution(872492545052850425)
XLA Ops:
  7.2 0.8 reduce
  8.4 3.0 fusion.12
  11.7 1.3 fusion.22
  14.0 4.2 stack.41
  18.2 12.6 %all-to-all-start = ((bf16[64,256,256]{2,1,0:T(8,128)(2,1)}), bf16[64,256,256]{2,1,0:T(8,128)(2,1)}, u32[]{:S(2)}, u32[]{:S(2)}) async-start(bf16[64,256,256]{2,1,0:T(8,128)(2,1)} %stack.41), calls=%async_computation | async-start | bytes 16777216 | tf_op jit(solution)/shard_map/all_to_all | solution.py:146
  30.9 0.7 slice.128
  31.6 0.7 slice.129
  38.2 0.7 broadcast_in_dim_reshape.2
  39.0 0.7 all_to_all.13
  39.7 0.7 copy.44
  40.4 0.9 bitcast_dynamic-update-slice_fusion.11
  41.3 0.9 bitcast_dynamic-update-slice_fusion.10
  42.2 0.9 bitcast_dynamic-update-slice_fusion.9
  43.2 0.9 bitcast_dynamic-update-slice_fusion.8
  44.1 0.9 bitcast_dynamic-update-slice_fusion.7
  45.0 0.9 bitcast_dynamic-update-slice_fusion.6
  46.0 0.9 bitcast_dynamic-update-slice_fusion.3
  46.9 0.9 bitcast_dynamic-update-slice_fusion.2
  47.8 0.9 bitcast_dynamic-update-slice_fusion.1
  48.7 0.9 bitcast_dynamic-update-slice_fusion
  49.7 1.9 fusion.32
  51.6 0.7 fusion.40
  52.3 0.7 multiply_reduce_fusion.1
  53.1 1.2 fusion.2
  54.8 1.2 copy-done.6
  56.0 2.3 copy.45
  58.3 2.5 reshape.247
  62.0 155.0 %all-to-all-done = bf16[64,256,256]{2,1,0:T(8,128)(2,1)} async-done(((bf16[64,256,256]{2,1,0:T(8,128)(2,1)}), bf16[64,256,256]{2,1,0:T(8,128)(2,1)}, u32[]{:S(2)}, u32[]{:S(2)}) %all-to-all-start) | async-done | bytes 8388640 | tf_op jit(solution)/shard_map/all_to_all | solution.py:146
  217.0 6.8 %all-to-all-start.1 = ((s32[64,1,2]{2,1,0:T(1,128)}), s32[64,1,2]{2,1,0:T(1,128)S(1)}, u32[]{:S(2)}, u32[]{:S(2)}) async-start(s32[64,1,2]{2,1,0:T(1,128)} %bitcast.38), calls=%async_computation.1 | async-start | bytes 65536 | tf_op jit(solution)/shard_map/all_to_all | solution.py:140
  223.8 10.6 %gather_fusion.2 = bf16[128,128,256]{2,1,0:T(8,128)(2,1)} fusion(bf16[64,2,128,256]{3,2,1,0:T(8,128)(2,1)} %bitcast.23, s32[128]{0:T(128)S(1)} %reshape.271), kind=kCustom, calls=%fused_computation.2 | custom fusion | bytes 16778240 | tf_op jit(solution)/shard_map/jit(take_along_axis)/gather | solution.py:151
  234.4 7.4 %broadcast_select_fusion = bf16[128,128,256]{2,1,0:T(8,128)(2,1)} fusion(bf16[128,128,256]{2,1,0:T(8,128)(2,1)} %gather_fusion.2, pred[128]{0:T(512)(128)(4,1)S(1)} %compare_and_fusion.1), kind=kLoop, calls=%fused_computation.5 | loop fusion | flops 4194304 | bytes 16777344 | tf_op jit(solution)/shard_map/jit(take_along_axis)/select_n | solution.py:151
  241.8 5.4 gather_fusion
  247.2 1.9 bitcast_select_fusion
  249.1 3.8 fusion.1
  253.4 3.6 divide_convert_fusion
  257.1 1.4 convolution_convert_fusion
  258.7 6.4 %gather_fusion.1 = bf16[128,128,256]{2,1,0:T(8,128)(2,1)} fusion(bf16[32,128,256]{2,1,0:T(8,128)(2,1)S(1)} %bitcast.125, s32[1024]{0:T(1024)S(1)} %get-tuple-element.28), kind=kCustom, calls=%fused_computation.1 | custom fusion | bytes 16777728 | tf_op jit(solution)/shard_map/jit(_take)/gather | solution.py:158
  265.1 7.4 %select_select_fusion = bf16[64,2,128,256]{3,2,1,0:T(8,128)(2,1)} fusion(bf16[64,2,128,256]{3,2,1,0:T(8,128)(2,1)} %bitcast.126, pred[64,2]{1,0:T(8,128)(4,1)S(1)} %compare_and_fusion, pred[64,2]{1,0:T(8,128)(4,1)S(1)} %broadcast_in_dim.116), kind=kLoop, calls=%fused_computation.4 | loop fusion | flops 8388608 | bytes 16777472 | tf_op jit(solution)/shard_map/jit(_where)/select_n | solution.py:159
  272.5 10.9 %all-to-all-start.2 = ((bf16[64,2,128,256]{3,2,1,0:T(8,128)(2,1)}), bf16[64,2,128,256]{3,2,1,0:T(8,128)(2,1)}, u32[]{:S(2)}, u32[]{:S(2)}) async-start(bf16[64,2,128,256]{3,2,1,0:T(8,128)(2,1)} %select_select_fusion), calls=%async_computation.2 | async-start | bytes 16777216 | tf_op jit(solution)/shard_map/all_to_all | solution.py:162
  284.2 0.7 reduce.8
  285.1 4.2 fusion.105
  289.3 4.8 reshape.252
  294.1 21.9 %divide_convert_fusion.1 = bf16[256,12,256]{2,0,1:T(8,128)(2,1)} fusion(f32[256,12]{0,1:T(8,128)S(1)} %add_sqrt_fusion, f32[256,12,256]{2,1,0:T(8,128)} %reshape.252, bf16[256,12,256]{2,0,1:T(8,128)(2,1)} %copy-done.12, f32[256,12]{0,1:T(8,128)S(1)} %get-tuple-element.18, f32[256,12,256]{2,0,1:T(8,128)S(1)} %copy-done.11), kind=kOutput, calls=%fused_computation.14 | output fusion | flops 10226943 | bytes 9461760 | tf_op jit(solution)/shard_map/mul | solution.py:111
  316.0 1.7 copy.53
  317.7 2.3 fusion.106
  320.5 0.7 slice_bitcast_fusion.10
  321.2 0.7 slice_bitcast_fusion.11
  322.0 0.7 slice_bitcast_fusion.7
  322.7 0.7 slice_bitcast_fusion.8
  323.4 0.7 slice_bitcast_fusion
  324.1 0.7 slice_bitcast_fusion.9
  324.8 0.7 slice_bitcast_fusion.1
  325.6 0.7 slice_bitcast_fusion.2
  326.3 0.7 slice_bitcast_fusion.3
  327.0 0.7 slice_bitcast_fusion.4
  327.7 0.7 slice_bitcast_fusion.5
  328.4 0.7 slice_bitcast_fusion.6
  329.1 248.6 %all-reduce.28.cloned.1.call-done = f32[256,3072]{1,0:T(8,128)} async-done(((f32[256,3072]{1,0:T(8,128)}), f32[256,3072]{1,0:T(8,128)}) %all-reduce.28.cloned.1.call-update) | async-done | bytes 3145744 | tf_op jit(solution)/shard_map/psum | solution.py:172
  577.7 2.1 broadcast_multiply_fusion
  579.9 2.4 copy.54
  582.2 3.7 copy.55
  586.0 12.3 %copy.58 = bf16[16,8,128,256]{3,1,2,0:T(8,128)(2,1)} copy(bf16[16,8,128,256]{3,2,1,0:T(8,128)(2,1)} %bitcast.52) | data formatting | bytes 16777216
  598.4 4.7 fusion.90
  603.5 2.1 multiply_bitcast_fusion
  (120 shorter events, 11.5 us)
Async XLA Ops:
  7.2 4.5 copy-start
  11.7 1.4 copy-start.24
  11.7 1.9 copy-start.27
  14.0 23.1 %copy-start.4 = (bf16[256,256]{1,0:T(8,128)(2,1)}, bf16[256,256]{1,0:T(8,128)(2,1)S(1)}, u32[]{:S(2)}) copy-start(bf16[256,256]{1,0:T(8,128)(2,1)S(1)} %fusion.34) | copy-start | bytes 393220
  18.2 19.5 %copy-start.26 = (s32[1,8,4,2]{1,3,2,0:T(2,128)S(1)}, s32[1,8,4,2]{1,3,2,0:T(2,128)}, u32[]{:S(2)}) copy-start(s32[1,8,4,2]{1,3,2,0:T(2,128)} %param.15) | copy-start | bytes 772
  18.2 198.7 %all-to-all-start = ((bf16[64,256,256]{2,1,0:T(8,128)(2,1)}), bf16[64,256,256]{2,1,0:T(8,128)(2,1)}, u32[]{:S(2)}, u32[]{:S(2)}) async-start(bf16[64,256,256]{2,1,0:T(8,128)(2,1)} %stack.41), calls=%async_computation | async-start | bytes 16777216 | tf_op jit(solution)/shard_map/all_to_all | solution.py:146
  30.9 8.8 %copy-start.13 = (bf16[256,12,256]{2,0,1:T(8,128)(2,1)S(1)}, bf16[256,12,256]{2,0,1:T(8,128)(2,1)}, u32[]{:S(2)}) copy-start(bf16[256,12,256]{2,0,1:T(8,128)(2,1)} %param.14) | copy-start | bytes 4718596
  37.7 8.2 %slice-start = ((bf16[256,256]{1,0:T(8,128)(2,1)}), bf16[248,256]{1,0:T(8,128)(2,1)S(1)}, s32[]{:S(2)}) async-start(bf16[256,256]{1,0:T(8,128)(2,1)} %copy-done.4), calls=%async_computation.4 | async-start | bytes 253952 | tf_op jit(solution)/shard_map/slice | solution.py:66
  49.6 3.5 copy-start.12
  49.6 2.0 copy-start.28
  53.1 1.7 copy-start.10
  54.8 1.2 copy-start.6
  56.0 4.7 copy-start.25
  60.8 188.4 %copy-start.8 = (bf16[8,384,256]{2,1,0:T(8,128)(2,1)}, bf16[8,384,256]{2,1,0:T(8,128)(2,1)S(1)}, u32[]{:S(2)}) copy-start(bf16[8,384,256]{2,1,0:T(8,128)(2,1)S(1)} %reshape.247) | copy-start | bytes 4718596
  217.0 55.6 %all-to-all-start.1 = ((s32[64,1,2]{2,1,0:T(1,128)}), s32[64,1,2]{2,1,0:T(1,128)S(1)}, u32[]{:S(2)}, u32[]{:S(2)}) async-start(s32[64,1,2]{2,1,0:T(1,128)} %bitcast.38), calls=%async_computation.1 | async-start | bytes 65536 | tf_op jit(solution)/shard_map/all_to_all | solution.py:140
  249.1 3.8 copy-start.5
  253.4 3.6 copy-start.9
  257.1 1.7 copy-start.2
  272.5 12.6 %copy-start.3 = (bf16[8,384,512]{2,1,0:T(8,128)(2,1)S(1)}, bf16[8,384,512]{2,1,0:T(8,128)(2,1)}, u32[]{:S(2)}) copy-start(bf16[8,384,512]{2,1,0:T(8,128)(2,1)} %copy-done.2) | copy-start | bytes 9437188
  272.5 313.4 %all-to-all-start.2 = ((bf16[64,2,128,256]{3,2,1,0:T(8,128)(2,1)}), bf16[64,2,128,256]{3,2,1,0:T(8,128)(2,1)}, u32[]{:S(2)}, u32[]{:S(2)}) async-start(bf16[64,2,128,256]{3,2,1,0:T(8,128)(2,1)} %select_select_fusion), calls=%async_computation.2 | async-start | bytes 16777216 | tf_op jit(solution)/shard_map/all_to_all | solution.py:162
  283.5 294.3 %all-reduce.28.cloned.1.call-start = ((), (), s32[]{:S(2)}) async-start(), calls=%async_computation.3 | async-start | bytes 6291456 | tf_op jit(solution)/shard_map/psum | solution.py:172
  289.3 4.8 copy-start.11
  317.7 2.3 copy-start.7
  598.3 5.0 copy-start.14
  598.3 5.1 copy-start.15
  598.3 5.1 copy-start.16
  598.3 5.1 copy-start.17
  598.3 5.1 copy-start.18
  598.3 5.1 copy-start.19
  598.3 5.1 copy-start.20
  598.3 5.1 copy-start.21
  598.4 5.1 copy-start.22
  598.4 5.1 copy-start.23
  598.4 7.2 %copy-start.1 = (bf16[512,256]{1,0:T(8,128)(2,1)S(1)}, bf16[512,256]{1,0:T(8,128)(2,1)}, u32[]{:S(2)}) copy-start(bf16[512,256]{1,0:T(8,128)(2,1)} %param.10) | copy-start | bytes 786436
Sparse Core Ops, SparseCore 0:
  320.1 257.5 all-reduce.27
